TPU v7x, 32 devices: a whole 2x2x4 slice. The times are simulated.
32 devices in a mesh: groups: 2 (over y), store: 4 (over z), mp: 4 (over x, core).
Axes of the slice: x: 2, y: 2, z: 4, core: 2. Of those that a mesh axis runs over, the one named last changes fastest.
Arguments:
- hidden: bfloat16 [8, 128, 4096], P(('groups', 'store')), parts along dimension 0, may hold values from -6 to 6
- query_weight: bfloat16 [4096, 8192], P('store', 'mp'), may hold values from -0.09375 to 0.09375
- keyvalue_weight: bfloat16 [4096, 2048], P('store', 'mp'), may hold values from -0.09375 to 0.09375
- block_store: bfloat16 [128, 1024, 2048], P('groups', 'store', 'mp'), parts along dimension 0, may hold values from -256 to 256
- block_ids: int32 [8, 4], P('groups'), parts along dimension 0, may hold values from 0 to 63, as said below
- offsets: int32 [8, 4], P('groups'), parts along dimension 0, may hold values from 0 to 3135, as said below
- served: int32 [8], P('groups'), parts along dimension 0, may hold values from 0 to 3, each once
Outputs:
- attended: bfloat16 [8, 128, 8192], P(('groups', 'store'), None, 'mp'), parts along dimension 0
There are 2 independent parts, one for each index of `groups`. A program takes and returns all parts, laid end to end along the dimension named above; an argument that names none is the same for every part. Nothing has to cross between parts.
Inputs may be any that keep to these rules, and one draw needn't show every extreme that they name: `block_ids`: the 4 block ids of one request differ. `offsets`: block c of a request starts at c * 1024 plus 0 to 63.
All inputs are finite; a program needn't handle non-finite values.
Results may differ from a plain program's by a relative error of at most 0.004.
The roundings to bfloat16 on the way count: a program that leaves them out, or rounds other values in their place, can miss the bound.
Values may be sent and summed in bfloat16 or wider, within the bound.
A program may use at most 128 MiB of HBM per device.

v0:
```python
import math
import jax
import jax.numpy as jnp
from jax import lax
from jax.sharding import PartitionSpec as P

HD = 128
NCH = 4
L = 1024
GAP = 64


def rotary_tables(positions, head_size):
    half_size = head_size // 2
    freq_index = jnp.arange(half_size, dtype=jnp.float32)
    inverse = jnp.exp(freq_index * (-2.0 * math.log(500000.0) / head_size))
    period = jnp.floor(2.0 * math.pi / inverse + 0.5)
    position_f = positions.astype(jnp.float32)[:, None]
    angles = jnp.mod(position_f, period[None, :]) / period[None, :] * (2.0 * math.pi)
    return (jnp.cos(angles), jnp.sin(angles))


def rotate(values, cosine, sine_values):
    half_size = values.shape[-1] // 2
    first_half = values[..., :half_size]
    second_half = values[..., half_size:]
    cos_b = cosine[:, None, :]
    sin_b = sine_values[:, None, :]
    return jnp.concatenate(
        [first_half * cos_b - second_half * sin_b, second_half * cos_b + first_half * sin_b],
        axis=-1,
    )


def rerotate(page_data, positions, head_size):
    page_rows = page_data.shape[0]
    split_view = page_data.reshape(page_rows, -1, 2, head_size)
    cosine, sine_values = rotary_tables(positions, head_size)
    turned = rotate(split_view[:, :, 0, :].astype(jnp.float32), cosine, sine_values).astype(
        jnp.bfloat16
    )
    return jnp.stack([turned, split_view[:, :, 1, :]], axis=2).reshape(page_rows, -1)


def attend(queries, cached_keys, cached_values, new_keys, new_values):
    row_count = queries.shape[0]
    head_count = queries.shape[1]
    sharing = head_count // cached_keys.shape[1]
    scaling = 1.0 / math.sqrt(queries.shape[2])
    causal = jnp.arange(row_count)[:, None] >= jnp.arange(row_count)[None, :]

    def one_head(head_index):
        kv_index = head_index // sharing
        q_one = lax.dynamic_index_in_dim(queries, head_index, 1, keepdims=False)
        k_old = lax.dynamic_index_in_dim(cached_keys, kv_index, 1, keepdims=False)
        v_old = lax.dynamic_index_in_dim(cached_values, kv_index, 1, keepdims=False)
        k_new = lax.dynamic_index_in_dim(new_keys, kv_index, 1, keepdims=False)
        v_new = lax.dynamic_index_in_dim(new_values, kv_index, 1, keepdims=False)
        past_scores = jnp.dot(q_one, k_old.T, preferred_element_type=jnp.float32) * scaling
        own_scores = jnp.dot(q_one, k_new.T, preferred_element_type=jnp.float32) * scaling
        own_scores = jnp.where(causal, own_scores, -jnp.inf)
        row_top = jnp.maximum(jnp.max(past_scores, axis=1), jnp.max(own_scores, axis=1))[:, None]
        w_old = jnp.exp(past_scores - row_top)
        w_new = jnp.exp(own_scores - row_top)
        denominator = jnp.sum(w_old, axis=1) + jnp.sum(w_new, axis=1)
        mixed = jnp.dot(w_old.astype(jnp.bfloat16), v_old, preferred_element_type=jnp.float32)
        mixed = mixed + jnp.dot(
            w_new.astype(jnp.bfloat16), v_new, preferred_element_type=jnp.float32
        )
        return (mixed / denominator[:, None]).astype(jnp.bfloat16)

    per_head = lax.map(one_head, jnp.arange(head_count, dtype=jnp.int32))
    return jnp.transpose(per_head, (1, 0, 2)).reshape(row_count, head_count * queries.shape[2])


def per_device(hidden, query_weight, keyvalue_weight, block_store, block_ids, offsets, served):
    tokens = hidden[0]
    row_count = tokens.shape[0]
    q_cols = query_weight.shape[1]
    kv_cols = keyvalue_weight.shape[1]
    head_count = q_cols // HD
    kv_heads = kv_cols // (2 * HD)

    def add_rows(panel):
        return jnp.dot(tokens, panel, preferred_element_type=jnp.float32)

    my_index = lax.axis_index("store")
    slot_count = lax.axis_size("store")
    share_rows = block_store.shape[1]
    wanted = block_ids[served]
    sending = jnp.take(block_store, wanted.reshape(-1), axis=0).reshape(
        slot_count * NCH * share_rows, kv_cols
    )
    sending = sending.reshape(slot_count, NCH, share_rows, kv_cols)
    queries = add_rows(lax.all_gather(query_weight, "store", axis=0, tiled=True))
    fresh_proj = add_rows(lax.all_gather(keyvalue_weight, "store", axis=0, tiled=True))
    received = lax.all_to_all(sending, "store", split_axis=0, concat_axis=2, tiled=True)
    received = received.reshape(NCH * L, kv_cols)
    request = served[my_index]
    key_pos = (offsets[request][:, None] + jnp.arange(L, dtype=jnp.int32)[None, :]).reshape(NCH * L)
    received = rerotate(received, key_pos, HD)
    split_pages = received.reshape(NCH * L, kv_heads, 2, HD)
    query_pos = NCH * L + GAP + jnp.arange(row_count, dtype=jnp.int32)
    cos_query, sin_query = rotary_tables(query_pos, HD)
    queries = rotate(queries.reshape(row_count, head_count, HD), cos_query, sin_query).astype(
        jnp.bfloat16
    )
    fresh_proj = fresh_proj.reshape(row_count, kv_heads, 2, HD)
    new_keys = rotate(fresh_proj[:, :, 0, :], cos_query, sin_query).astype(jnp.bfloat16)
    new_values = fresh_proj[:, :, 1, :].astype(jnp.bfloat16)
    attended = attend(
        queries, split_pages[:, :, 0, :], split_pages[:, :, 1, :], new_keys, new_values
    )
    return attended[None]


def solution(mesh):
    in_specs = (
        P(("groups", "store"), None, None),
        P("store", "mp"),
        P("store", "mp"),
        P("groups", "store", "mp"),
        P("groups", None),
        P("groups", None),
        P("groups"),
    )
    out_specs = P(("groups", "store"), None, "mp")
    return jax.shard_map(
        per_device, mesh=mesh, in_specs=in_specs, out_specs=out_specs, check_vma=False
    )
```

profile of v0, /device:TPU:0, one launch (start us, length us, event | category | flops | bytes accessed | tf_op | source)
XLA Modules:
  0.0 644.8 jit_solution(6617780340946554539)
XLA Ops:
  8.7 8.5 %gather_fusion.1 = bf16[16,256,512]{2,1,0:T(8,128)(2,1)} fusion(bf16[64,256,512]{2,1,0:T(8,128)(2,1)} %param.12, s32[1024]{0:T(1024)S(1)} %pad_clamp_fusion), kind=kCustom, calls=%fused_computation.1 | custom fusion | bytes 8388672 | tf_op jit(solution)/shard_map/jit(_take)/gather | solution.py:91
  17.3 5.0 broadcast_select_fusion
  22.3 6.3 all-to-all-start
  32.3 10.7 %fusion.41 = (f32[4096,64]{1,0:T(8,128)}, f32[4096,64]{1,0:T(8,128)}) fusion(pred[64]{0:T(512)(128)(4,1)S(1)} %broadcast_compare_fusion, f32[64]{0:T(128)S(1)} %add_floor_fusion, f32[4096]{0:T(1024)S(1)} %bitcast.99), kind=kLoop, calls=%fused_computation.56 | loop fusion | flops 2359296 | bytes 2113856 | tf_op jit(solution)/shard_map/cos | solution.py:20
  43.0 124.6 %all-gather.5.cloned.1.call-done = bf16[4096,512]{1,0:T(8,128)(2,1)} async-done(((bf16[1024,512]{1,0:T(8,128)(2,1)}), bf16[4096,512]{1,0:T(8,128)(2,1)}) %all-gather.5.cloned.1.call-update) | async-done | bytes 4194320 | tf_op jit(solution)/shard_map/all_gather | solution.py:96
  167.6 6.4 copy.36
  174.0 7.6 %all-to-all-done = bf16[4,4,256,512]{3,2,1,0:T(8,128)(2,1)} async-done(((bf16[4,4,256,512]{3,2,1,0:T(8,128)(2,1)}), bf16[4,4,256,512]{3,2,1,0:T(8,128)(2,1)}, u32[]{:S(2)}, u32[]{:S(2)}) %all-to-all-start) | async-done | bytes 4194336 | tf_op jit(solution)/shard_map/all_to_all | solution.py:97
  181.6 4.9 copy.35
  186.6 7.0 %reshape_reshape.4 = bf16[4096,2,2,128]{3,2,1,0:T(2,128)(2,1)} reshape(bf16[1,4,4,256,512]{4,3,2,1,0:T(8,128)(2,1)} %copy.35) | data formatting | bytes 8388608 | tf_op jit(solution)/shard_map/reshape;reshape | solution.py:37
  193.5 8.7 %fusion.52 = (bf16[4096,2,1,128]{3,2,1,0:T(2,128)(2,1)S(1)}, f32[4096,2,1,128]{3,2,1,0:T(1,128)S(1)}) fusion(bf16[4096,2,2,128]{3,2,1,0:T(2,128)(2,1)} %reshape_reshape.4), kind=kLoop, calls=%fused_computation.91 | loop fusion | flops 1048576 | bytes 10485760 | tf_op jit(solution)/shard_map/slice | solution.py:42
  204.5 11.2 %subtract_convert_fusion = (bf16[4096,2,64]{2,1,0:T(2,128)(2,1)S(1)}, bf16[4096,2,64]{2,1,0:T(2,128)(2,1)S(1)}) fusion(f32[4096,2,128]{2,1,0:T(2,128)S(1)} %bitcast.92, f32[4096,64]{1,0:T(8,128)S(1)} %copy-done.3, f32[4096,64]{1,0:T(8,128)S(1)} %copy-done.2), kind=kLoop, calls=%fused_computation.43 | loop fusion | flops 4194304 | bytes 8388608 | tf_op jit(solution)/shard_map/convert.4
  215.7 5.7 pad_maximum_fusion
  225.7 228.4 %all-gather.3.cloned.1.call-done = bf16[4096,2048]{1,0:T(8,128)(2,1)} async-done(((bf16[1024,2048]{1,0:T(8,128)(2,1)}), bf16[4096,2048]{1,0:T(8,128)(2,1)}) %all-gather.3.cloned.1.call-update) | async-done | bytes 16777232 | tf_op jit(solution)/shard_map/all_gather | solution.py:95
  454.1 20.7 %copy.34 = bf16[2048,4096]{1,0:T(8,128)(2,1)} copy(bf16[2048,4096]{0,1:T(8,128)(2,1)} %bitcast.94) | data formatting | bytes 33554432 | tf_op jit(solution)/shard_map/dot_general | solution.py:85
  474.8 8.1 %fusion.38 = f32[128,16,128]{0,2,1:T(8,128)S(1)} fusion(bf16[16,128,4096]{2,1,0:T(8,128)(2,1)} %bitcast.91, bf16[1,128,4096]{2,1,0:T(8,128)(2,1)S(1)} %copy-done), kind=kOutput, calls=%fused_computation.53 | convolution fusion | flops 2147483648 | bytes 18874368 | tf_op jit(solution)/shard_map/dot_general | solution.py:85
  483.9 151.7 %while.13 = (s32[]{:T(128)}, bf16[16,128,128]{2,1,0:T(8,128)(2,1)}, s32[16]{0:T(128)S(1)}, bf16[128,16,128]{0,2,1:T(8,128)(2,1)}, bf16[4096,2,128]{2,0,1:T(8,128...) while((s32[]{:T(128)}, bf16[16,128,128]{2,1,0:T(8,128)(2,1)}, ...), condition=%wide.region_5.6_spmd.clone, body=%wide.region_0.5_spmd.clone.sunk | while | flops 280149760 | bytes 8888206 | solution.py:72
  489.7 1.8 fusion.69
  499.2 1.8 fusion.69
  508.7 1.8 fusion.69
  527.6 1.8 fusion.69
  537.1 1.8 fusion.69
  546.6 1.8 fusion.69
  565.6 1.8 fusion.69
  575.0 1.8 fusion.69
  (180 shorter events, 84.2 us)
Async XLA Ops:
  6.5 216.5 %copy-start = (bf16[1,128,4096]{2,1,0:T(8,128)(2,1)S(1)}, bf16[1,128,4096]{2,1,0:T(8,128)(2,1)}, u32[]{:S(2)}) copy-start(bf16[1,128,4096]{2,1,0:T(8,128)(2,1)} %param.9) | copy-start | bytes 3145732
  6.5 161.1 %all-gather.5.cloned.1.call-start = ((), (), s32[]{:S(2)}) async-start(), calls=%async_computation.2 | async-start | bytes 5242880 | tf_op jit(solution)/shard_map/all_gather | solution.py:96
  7.3 0.8 copy-start.5
  7.3 0.8 copy-start.4
  7.3 446.8 %all-gather.3.cloned.1.call-start = ((), (), s32[]{:S(2)}) async-start(), calls=%async_computation.1 | async-start | bytes 20971520 | tf_op jit(solution)/shard_map/all_gather | solution.py:95
  22.3 159.4 %all-to-all-start = ((bf16[4,4,256,512]{3,2,1,0:T(8,128)(2,1)}), bf16[4,4,256,512]{3,2,1,0:T(8,128)(2,1)}, u32[]{:S(2)}, u32[]{:S(2)}) async-start(bf16[4,4,256,512]{3,2,1,0:T(8,128)(2,1)} %broadcast_select_fusion), calls=%async_computation | async-start | bytes 8388608 | tf_op jit(solution)/shard_map/all_to_all | solution.py:97
  202.3 1.6 copy-start.2
  202.3 2.2 copy-start.3
  221.4 3.0 copy-start.1
Sparse Core Ops, SparseCore 0:
  8.9 158.6 all-gather.4
  169.2 284.8 all-gather.2
where the time goes:
time: 648 us; the launch traced here: 645 us
  waiting for transfers between devices  362 us (56%)
  matrix products  75.7 us (12%)
  local copies, waits for them, and re-layouts  67.7 us (10%)
  loops' own time  66.9 us (10%)
  other arithmetic  50.6 us (8%)
  between operations  15.7 us (2%)
    all_gather x1, waiting for transfers between devices, per_device(): lax.all_gather(query_weight, 'store', axis=0, tiled=True)  228 us
    all_gather x1, waiting for transfers between devices, per_device(): lax.all_gather(keyvalue_weight, 'store', axis=0, tiled=True)  125 us
    another operation x1, loops' own time, attend(): per_head = lax.map(one_head, jnp.arange(head_count, dtype=jnp.int32))  66.9 us
    dot_general x16, matrix products, one_head(): jnp.dot(q_one, k_old.T, preferred_element_type=jnp.float32) * scaling  28.6 us
    dot_general x2, local copies, waits for them, and re-layouts, add_rows(): return jnp.dot(tokens, panel, preferred_element_type=jnp.float32)  27 us
    dot_general x16, matrix products, one_head(): jnp.dot(q_one, k_new.T, preferred_element_type=jnp.float32) * scaling  15.9 us
    dot_general x16, matrix products, one_head(): jnp.dot(w_new.astype(jnp.bfloat16), v_new, preferred_element_type=jnp.flo...  13.1 us
  transfers between devices with their start and end apart: 3, of which 3 were waited for; matrix products, arithmetic and copies ran while one was open for 11% of the time, Pallas kernels for 0%

commit v1 on v0

--- a/solution.py
+++ b/solution.py
@@ -8,6 +8,14 @@
 NCH = 4
 L = 1024
 GAP = 64
+
+
+def use_quotas(xx):
+    work_now = lax.axis_size("store")
+    all_values = jnp.stack(jnp.split(xx, work_now, axis=0), 0)
+    lower = lax.all_to_all(all_values, axis_name="store", split_axis=0, concat_axis=0)
+    item_now = jnp.concatenate(lower, 2)
+    return item_now
 
 
 def rotary_tables(positions, head_size):
@@ -94,7 +102,7 @@
     sending = sending.reshape(slot_count, NCH, share_rows, kv_cols)
     queries = add_rows(lax.all_gather(query_weight, "store", axis=0, tiled=True))
     fresh_proj = add_rows(lax.all_gather(keyvalue_weight, "store", axis=0, tiled=True))
-    received = lax.all_to_all(sending, "store", split_axis=0, concat_axis=2, tiled=True)
+    received = use_quotas(sending)
     received = received.reshape(NCH * L, kv_cols)
     request = served[my_index]
     key_pos = (offsets[request][:, None] + jnp.arange(L, dtype=jnp.int32)[None, :]).reshape(NCH * L)

time: 648 us -> 643 us (level)
    another operation x3 -> x4, other arithmetic: 11.3 us -> 13.6 us
  transfers between devices with their start and end apart: 3 -> 3, of which waited for: 3 -> 3; matrix products, arithmetic and copies ran while one was open for 11% -> 12% of each run, Pallas kernels for 0% -> 0%
where the time goes in v1:
time: 643 us; the launch traced here: 639 us
  waiting for transfers between devices  362 us (56%)
  matrix products  75.7 us (12%)
  local copies, waits for them, and re-layouts  66.9 us (10%)
  loops' own time  61.8 us (10%)
  other arithmetic  50.9 us (8%)
  between operations  15.6 us (2%)
    all_gather x1, waiting for transfers between devices, per_device(): lax.all_gather(query_weight, 'store', axis=0, tiled=True)  229 us
    all_gather x1, waiting for transfers between devices, per_device(): lax.all_gather(keyvalue_weight, 'store', axis=0, tiled=True)  124 us
    another operation x1, loops' own time, attend(): per_head = lax.map(one_head, jnp.arange(head_count, dtype=jnp.int32))  61.8 us
    dot_general x16, matrix products, one_head(): jnp.dot(q_one, k_old.T, preferred_element_type=jnp.float32) * scaling  28.6 us
    dot_general x2, local copies, waits for them, and re-layouts, add_rows(): return jnp.dot(tokens, panel, preferred_element_type=jnp.float32)  27.3 us
    dot_general x16, matrix products, one_head(): jnp.dot(q_one, k_new.T, preferred_element_type=jnp.float32) * scaling  15.9 us
    dot_general x16, matrix products, one_head(): jnp.dot(w_new.astype(jnp.bfloat16), v_new, preferred_element_type=jnp.flo...  13.1 us
  transfers between devices with their start and end apart: 3, of which 3 were waited for; matrix products, arithmetic and copies ran while one was open for 12% of the time, Pallas kernels for 0%

profile of v1, /device:TPU:0, one launch (start us, length us, event | category | flops | bytes accessed | tf_op | source)
XLA Modules:
  0.0 639.4 jit_solution(4198272486620178831)
XLA Ops:
  8.8 8.5 %gather_fusion.1 = bf16[16,256,512]{2,1,0:T(8,128)(2,1)} fusion(bf16[64,256,512]{2,1,0:T(8,128)(2,1)} %param.12, s32[1024]{0:T(1024)S(1)} %pad_clamp_fusion), kind=kCustom, calls=%fused_computation.1 | custom fusion | bytes 8388672 | tf_op jit(solution)/shard_map/jit(_take)/gather | solution.py:99
  17.4 3.1 broadcast_select_fusion
  20.8 2.3 pad_maximum_fusion
  23.1 6.2 all-to-all-start
  33.1 10.7 %fusion.41 = (f32[4096,64]{1,0:T(8,128)}, f32[4096,64]{1,0:T(8,128)}) fusion(pred[64]{0:T(512)(128)(4,1)S(1)} %broadcast_compare_fusion, f32[64]{0:T(128)S(1)} %add_floor_fusion, f32[4096]{0:T(1024)S(1)} %bitcast.103), kind=kLoop, calls=%fused_computation.61 | loop fusion | flops 2359296 | bytes 2113856 | tf_op jit(solution)/shard_map/cos | solution.py:28
  43.8 123.6 %all-gather.5.cloned.1.call-done = bf16[4096,512]{1,0:T(8,128)(2,1)} async-done(((bf16[1024,512]{1,0:T(8,128)(2,1)}), bf16[4096,512]{1,0:T(8,128)(2,1)}) %all-gather.5.cloned.1.call-update) | async-done | bytes 4194320 | tf_op jit(solution)/shard_map/all_gather | solution.py:104
  167.4 6.4 %copy.25 = bf16[512,4096]{1,0:T(8,128)(2,1)} copy(bf16[512,4096]{0,1:T(8,128)(2,1)} %bitcast.101) | data formatting | bytes 8388608 | tf_op jit(solution)/shard_map/dot_general | solution.py:93
  173.8 7.8 %all-to-all-done = bf16[4,1,4,256,512]{4,3,2,1,0:T(8,128)(2,1)} async-done(((bf16[4,1,4,256,512]{4,3,2,1,0:T(8,128)(2,1)}), bf16[4,1,4,256,512]{4,3,2,1,0:T(8,128)(2,1)}, u32[]{:S(2)}, u32[]{:S(2)}) %all-to-all-start) | async-done | bytes 4194336 | tf_op jit(solution)/shard_map/all_to_all | solution.py:16
  181.6 4.9 copy.24
  186.6 7.0 %reshape_reshape_reshape.3 = bf16[4096,2,2,128]{3,2,1,0:T(2,128)(2,1)} reshape(bf16[1,4,4,256,512]{4,3,2,1,0:T(8,128)(2,1)} %copy.24) | data formatting | bytes 8388608 | tf_op jit(solution)/shard_map/reshape;reshape;reshape | solution.py:45
  193.5 8.7 %fusion.52 = (bf16[4096,2,1,128]{3,2,1,0:T(2,128)(2,1)S(1)}, f32[4096,2,1,128]{3,2,1,0:T(1,128)S(1)}) fusion(bf16[4096,2,2,128]{3,2,1,0:T(2,128)(2,1)} %reshape_reshape_reshape.3), kind=kLoop, calls=%fused_computation.96 | loop fusion | flops 1048576 | bytes 10485760 | tf_op jit(solution)/shard_map/slice | solution.py:50
  204.5 11.2 %subtract_convert_fusion = (bf16[4096,2,64]{2,1,0:T(2,128)(2,1)S(1)}, bf16[4096,2,64]{2,1,0:T(2,128)(2,1)S(1)}) fusion(f32[4096,2,128]{2,1,0:T(2,128)S(1)} %bitcast.97, f32[4096,64]{1,0:T(8,128)S(1)} %copy-done.3, f32[4096,64]{1,0:T(8,128)S(1)} %copy-done.2), kind=kLoop, calls=%fused_computation.44 | loop fusion | flops 4194304 | bytes 8388608 | tf_op jit(solution)/shard_map/convert.4
  215.6 5.7 pad_maximum_fusion.1
  224.4 229.4 %all-gather.3.cloned.1.call-done = bf16[4096,2048]{1,0:T(8,128)(2,1)} async-done(((bf16[1024,2048]{1,0:T(8,128)(2,1)}), bf16[4096,2048]{1,0:T(8,128)(2,1)}) %all-gather.3.cloned.1.call-update) | async-done | bytes 16777232 | tf_op jit(solution)/shard_map/all_gather | solution.py:103
  453.8 20.9 %copy.23 = bf16[2048,4096]{1,0:T(8,128)(2,1)} copy(bf16[2048,4096]{0,1:T(8,128)(2,1)} %bitcast.99) | data formatting | bytes 33554432 | tf_op jit(solution)/shard_map/dot_general | solution.py:93
  474.7 8.1 %fusion.38 = f32[128,16,128]{0,2,1:T(8,128)S(1)} fusion(bf16[16,128,4096]{2,1,0:T(8,128)(2,1)} %bitcast.96, bf16[1,128,4096]{2,1,0:T(8,128)(2,1)S(1)} %copy-done), kind=kOutput, calls=%fused_computation.58 | convolution fusion | flops 2147483648 | bytes 18874368 | tf_op jit(solution)/shard_map/dot_general | solution.py:93
  483.8 146.4 %while.13 = (s32[]{:T(128)}, bf16[16,128,128]{2,1,0:T(8,128)(2,1)}, s32[16]{0:T(128)S(1)}, bf16[128,16,128]{0,2,1:T(8,128)(2,1)}, bf16[4096,2,128]{2,0,1:T(8,128...) while((s32[]{:T(128)}, bf16[16,128,128]{2,1,0:T(8,128)(2,1)}, ...), condition=%wide.region_5.6_spmd.clone, body=%wide.region_0.5_spmd.clone.sunk | while | flops 280149760 | bytes 8888206 | solution.py:80
  498.4 1.8 fusion.69
  507.6 1.8 fusion.69
  535.0 1.8 fusion.69
  544.2 1.8 fusion.69
  571.6 1.8 fusion.69
  580.8 1.8 fusion.69
  608.2 1.8 fusion.69
  (183 shorter events, 84.9 us)
Async XLA Ops:
  6.5 216.5 %copy-start = (bf16[1,128,4096]{2,1,0:T(8,128)(2,1)S(1)}, bf16[1,128,4096]{2,1,0:T(8,128)(2,1)}, u32[]{:S(2)}) copy-start(bf16[1,128,4096]{2,1,0:T(8,128)(2,1)} %param.9) | copy-start | bytes 3145732
  6.5 1.5 copy-start.5
  6.5 1.5 copy-start.4
  6.5 160.8 %all-gather.5.cloned.1.call-start = ((), (), s32[]{:S(2)}) async-start(), calls=%async_computation.2 | async-start | bytes 5242880 | tf_op jit(solution)/shard_map/all_gather | solution.py:104
  7.3 446.5 %all-gather.3.cloned.1.call-start = ((), (), s32[]{:S(2)}) async-start(), calls=%async_computation.1 | async-start | bytes 20971520 | tf_op jit(solution)/shard_map/all_gather | solution.py:103
  23.1 158.5 %all-to-all-start = ((bf16[4,1,4,256,512]{4,3,2,1,0:T(8,128)(2,1)}), bf16[4,1,4,256,512]{4,3,2,1,0:T(8,128)(2,1)}, u32[]{:S(2)}, u32[]{:S(2)}) async-start(bf16[4,1,4,256,512]{4,3,2,1,0:T(8,128)(2,1)} %pad_maximum_fusion), calls=%async_computation | async-start | bytes 8388608 | tf_op jit(solution)/shard_map/all_to_all | solution.py:16
  202.2 1.6 copy-start.2
  202.2 2.2 copy-start.3
  215.6 7.4 %copy-start.1 = (bf16[512,4096]{1,0:T(8,128)(2,1)S(1)}, bf16[512,4096]{1,0:T(8,128)(2,1)}, u32[]{:S(2)}) copy-start(bf16[512,4096]{1,0:T(8,128)(2,1)} %copy.25) | copy-start | bytes 12582916
Sparse Core Ops, SparseCore 0:
  8.9 158.3 all-gather.4
  168.9 284.8 all-gather.2
